TPU v7x, 32 devices: a whole 2x2x4 slice. The times are simulated.
32 devices in a mesh: gy: 8 (over y, x, core), gx: 4 (over z).
Axes of the slice: x: 2, y: 2, z: 4, core: 2. Of those that a mesh axis runs over, the one named last changes fastest.
Arguments:
- feat_a: float32 [512, 256, 128], P('gy', 'gx'), may hold values from -8 to 8
- feat_b: float32 [512, 256, 128], P('gy', 'gx'), may hold values from -8 to 8
- occ_a: int32 [512, 256], P('gy', 'gx'), may hold values from 0 to 1, as said below
- occ_b: int32 [512, 256], P('gy', 'gx'), may hold values from 0 to 1, as said below
- first_weight: bfloat16 [256, 256], replicated, may hold values from -0.375 to 0.375
- second_weight: bfloat16 [256, 128], replicated, may hold values from -0.375 to 0.375
Outputs:
- matched_a: float32 [512, 256, 128], P('gy', 'gx')
- matched_b: float32 [512, 256, 128], P('gy', 'gx')
Inputs may be any that keep to these rules, and one draw needn't show every extreme that they name: `occ_a`: 1 marks an occupied cell. `occ_b`: 1 marks an occupied cell.
All inputs are finite; a program needn't handle non-finite values.
Results may differ from a plain program's by a relative error of at most 0.0042.
Values may be sent and summed in bfloat16 or wider, within the bound.
A program may use at most 64 MiB of HBM per device.

v0:
```python
import functools

import jax
import jax.numpy as jnp
import numpy as np
from jax import lax
from jax.experimental import pallas as pl
from jax.experimental.pallas import tpu as pltpu
from jax.sharding import PartitionSpec as P

R = 8
band = 8
tile_width = 16
key_rows = band + 2 * R
key_width = tile_width + 2 * R
BLOCKED = -1e30
OCC_LANE = band + tile_width
ONE_LANE = OCC_LANE + 1


def extended(cells, sides, width):
    for axis, dim in sides:
        count = lax.axis_size(axis)
        ends = count - 1
        head = lax.slice_in_dim(cells, 0, width, axis=dim)
        tail = lax.slice_in_dim(cells, cells.shape[dim] - width, cells.shape[dim], axis=dim)
        cells = jnp.concatenate(
            [
                lax.ppermute(tail, axis, [(i, (i + 1) % count) for i in range(ends)]),
                cells,
                lax.ppermute(head, axis, [((i + 1) % count, i) for i in range(ends)]),
            ],
            axis=dim,
        )
    return cells


def band_lanes(channels):
    keys = np.zeros((key_rows, key_width, channels), np.float32)
    down = np.arange(key_rows)
    side = np.arange(key_width)
    for i in range(band):
        keys[(down < i) | (down > i + 2 * R), :, i] = BLOCKED
    for i in range(tile_width):
        keys[:, (side < i) | (side > i + 2 * R), band + i] = BLOCKED
    keys[:, :, ONE_LANE] = 1.0
    queries = np.zeros((band, tile_width, channels), np.float32)
    for i in range(band):
        queries[i, :, i] = 1.0
    for i in range(tile_width):
        queries[:, i, band + i] = 1.0
    queries[:, :, OCC_LANE] = 1.0
    return (
        jnp.asarray(queries.reshape(-1, channels), jnp.bfloat16),
        jnp.asarray(keys.reshape(-1, channels), jnp.bfloat16),
    )


def gelu(x):
    size = jnp.abs(x)
    t = 1.0 / (1.0 + (0.3275911 * 0.5**0.5) * size)
    series = 0.5 * 1.061405429
    for a in (-1.453152027, 1.421413741, -0.284496736, 0.254829592):
        series = series * t + 0.5 * a
    tail = series * t * jnp.exp2((-0.5 / np.log(2.0)) * (x * x))
    return jnp.maximum(x, 0.0) - size * tail


def one_tile(feat, keys, bias, cell_mask, query_lanes, first, second):
    channels = feat.shape[-1]
    rate = 1.0 / (channels**0.5 * np.log(2.0))
    half = feat.astype(jnp.bfloat16)
    queries = jnp.concatenate([half, query_lanes], axis=1)
    wide = jnp.concatenate([keys, bias], axis=1)
    scores = lax.dot_general(
        queries, wide, (((1,), (1,)), ((), ())), preferred_element_type=jnp.float32
    )
    highest = jnp.maximum(jnp.max(scores, axis=1, keepdims=True), 0.0)
    exponent = jnp.exp2((scores - highest) * rate).astype(jnp.bfloat16)
    total = jnp.dot(exponent, wide, preferred_element_type=jnp.float32)
    denominator = jnp.exp2(-highest * rate) + total[:, channels + ONE_LANE : channels + ONE_LANE + 1]
    carried = (total[:, :channels] * (1.0 / denominator)).astype(jnp.bfloat16)
    joined = jnp.concatenate([half, carried], axis=1)
    hidden = gelu(jnp.dot(joined, first, preferred_element_type=jnp.float32)).astype(jnp.bfloat16)
    update = jnp.dot(hidden, second, preferred_element_type=jnp.float32)
    return feat + cell_mask.astype(jnp.float32) * update


def pass_kernel(
    feat_a, feat_b, mask_a, mask_b, keys_a, keys_b, bias_a, bias_b, query_lanes, key_lanes,
    first, second, *outs,
):
    top = pl.multiple_of(pl.program_id(0) * band, band)
    channels = feat_a.shape[-1]

    def cells(ref, left):
        return ref[:, pl.ds(left, tile_width), :].reshape(-1, channels)

    def window(ref, left):
        return ref[pl.ds(top, key_rows), pl.ds(left, key_width), :].reshape(-1, channels)

    def step(tile, carry):
        left = pl.multiple_of(tile * tile_width, tile_width)
        for i, (feat, keys, bias, mask) in enumerate(
            ((feat_a, keys_b, bias_b, mask_a), (feat_b, keys_a, bias_a, mask_b))
        ):
            new = one_tile(
                cells(feat, left),
                window(keys, left),
                window(bias, left) + key_lanes[...],
                cells(mask, left),
                query_lanes[...],
                first[...],
                second[...],
            ).reshape(band, tile_width, channels)
            outs[i][:, pl.ds(left, tile_width), :] = new
            if len(outs) > 2:
                outs[i + 2][:, pl.ds(left, tile_width), :] = new.astype(jnp.bfloat16)
        return carry

    lax.fori_loop(0, feat_a.shape[1] // tile_width, step, 0)


def one_pass(feats, masks, keys, biases, weights, halves):
    rows, cols, channels = feats[0].shape
    query_lanes, key_lanes = band_lanes(channels)
    strip = pl.BlockSpec((band, cols, channels), lambda i: (i, 0, 0))

    def whole(x):
        return pl.BlockSpec(x.shape, lambda i: (0,) * x.ndim)

    rest = (*keys, *biases, query_lanes, key_lanes, *weights)
    out_shape = [jax.ShapeDtypeStruct(feats[0].shape, jnp.float32)] * 2
    if halves:
        out_shape += [jax.ShapeDtypeStruct(feats[0].shape, jnp.bfloat16)] * 2
    return pl.pallas_call(
        pass_kernel,
        grid=(rows // band,),
        in_specs=[strip] * 4 + [whole(x) for x in rest],
        out_specs=[strip] * len(out_shape),
        out_shape=out_shape,
        compiler_params=pltpu.CompilerParams(vmem_limit_bytes=56 * 2**20),
    )(*feats, *masks, *rest)


def halo(half_a, half_b):
    both = extended(jnp.stack([half_a, half_b]), (("gy", 1), ("gx", 2)), R)
    return both[0], both[1]


def spread(mask, lane_values):
    return (mask[..., None] * lane_values).astype(jnp.bfloat16)


def local(feat_a, feat_b, occ_a, occ_b, first_weight, second_weight):
    channels = feat_a.shape[-1]
    weights = (first_weight, second_weight)
    feats = (feat_a, feat_b)
    ones = jnp.ones((channels,), jnp.bfloat16)
    masks = tuple(spread(occ.astype(jnp.bfloat16), ones) for occ in (occ_a, occ_b))
    occs = halo(occ_a.astype(jnp.bfloat16), occ_b.astype(jnp.bfloat16))
    lane = jnp.where(jnp.arange(channels) == OCC_LANE, BLOCKED, 0.0).astype(jnp.bfloat16)
    biases = tuple(spread(1 - occ, lane) for occ in occs)
    keys = halo(feat_a.astype(jnp.bfloat16), feat_b.astype(jnp.bfloat16))
    new_a, new_b, half_a, half_b = one_pass(feats, masks, keys, biases, weights, True)
    keys = halo(half_a, half_b)
    return tuple(one_pass((new_a, new_b), masks, keys, biases, weights, False))


def solution(mesh):
    in_specs = (P("gy", "gx", None), P("gy", "gx", None), P("gy", "gx"), P("gy", "gx"), P(), P())
    out_specs = (P("gy", "gx", None), P("gy", "gx", None))
    return jax.shard_map(local, mesh=mesh, in_specs=in_specs, out_specs=out_specs, check_vma=False)
```

profile of v0, /device:TPU:3, one launch (start us, length us, event | category | flops | bytes accessed | tf_op | source)
XLA Modules:
  0.0 197.0 jit_solution(14790358266365411442)
XLA Ops:
  0.6 0.8 convert_bitcast_fusion.2
  1.4 0.8 convert_bitcast_fusion.3
  2.2 3.7 %collective-permute-start.4 = (bf16[2,8,64]{2,1,0:T(8,128)(2,1)S(1)}, bf16[2,8,64]{2,1,0:T(8,128)(2,1)S(1)}, u32[]{:S(2)}, u32[]{:S(2)}) collective-permute-start(bf16[2,8,64]{2,1,0:T(8,128)(2,1)S(1)} %get-tuple-element.26), channel_id=1, source_target_pairs={{0,4},{4,8},{8,12},{12,16},{16,20},{20,24},{24,28},{1,5},{5,9},{9,... | collective-permute-start | bytes 6152 | tf_op jit(solution)/shard_map/ppermute | solution.py:29
  5.9 0.0 copy-start.2
  5.9 0.0 copy-start.3
  5.9 1.9 collective-permute-start.5
  7.8 2.7 %convert_bitcast_fusion = (bf16[1,64,64,128]{3,2,1,0:T(8,128)(2,1)S(1)}, bf16[1,64,64,128]{3,2,1,0:T(8,128)(2,1)S(1)}) fusion(f32[64,64,128]{2,1,0:T(8,128)} %feat_b.1, f32[64,64,128]{2,1,0:T(8,128)} %feat_a.1), kind=kLoop, calls=%fused_computation.6 | loop fusion | flops 1048576 | bytes 6291456 | tf_op jit(solution)/shard_map/stack | solution.py:147
  10.6 4.5 %collective-permute-start = (bf16[2,8,64,128]{3,2,1,0:T(8,128)(2,1)S(1)}, bf16[2,8,64,128]{3,2,1,0:T(8,128)(2,1)S(1)}, u32[]{:S(2)}, u32[]{:S(2)}) collective-permute-start(bf16[2,8,64,128]{3,2,1,0:T(8,128)(2,1)S(1)} %get-tuple-element.20), channel_id=1, source_target_pairs={{0,4},{4,8},{8,12},{12,16},{16,20},{20,24},{24,28},{1,5},{5,9},{9,... | collective-permute-start | bytes 786440 | tf_op jit(solution)/shard_map/ppermute | solution.py:29
  15.1 1.9 collective-permute-start.1
  17.1 0.0 collective-permute-done.4
  17.1 0.0 collective-permute-done.5
  17.1 0.1 fusion.3
  17.2 3.2 %collective-permute-start.6 = (bf16[2,80,8]{2,1,0:T(8,128)(2,1)S(1)}, bf16[2,80,8]{2,1,0:T(8,128)(2,1)S(1)}, u32[]{:S(2)}, u32[]{:S(2)}) collective-permute-start(bf16[2,80,8]{2,1,0:T(8,128)(2,1)S(1)} %get-tuple-element.24), channel_id=1, source_target_pairs={{0,1},{1,2},{2,3},{4,5},{5,6},{6,7},{8,9},{9,10},{10,11},{12,13},{... | collective-permute-start | bytes 7688 | tf_op jit(solution)/shard_map/ppermute | solution.py:29
  20.4 1.3 collective-permute-start.7
  21.7 0.0 copy-done.2
  21.7 0.0 copy-done.3
  21.7 0.0 collective-permute-done.6
  21.8 3.4 %collective-permute-done.7 = bf16[2,80,8]{2,1,0:T(8,128)(2,1)S(1)} collective-permute-done((bf16[2,80,8]{2,1,0:T(8,128)(2,1)S(1)}, bf16[2,80,8]{2,1,0:T(8,128)(2,1)S(1)}, u32[]{:S(2)}, u32[]{:S(2)}) %collective-permute-start.7) | collective-permute-done | bytes 2592 | tf_op jit(solution)/shard_map/ppermute | solution.py:31
  25.1 0.1 pad_maximum_fusion.15
  25.2 0.0 collective-permute-done
  25.2 0.0 collective-permute-done.1
  25.3 0.1 pad_maximum_fusion.9
  25.4 3.2 %collective-permute-start.2 = (bf16[2,80,8,128]{3,2,1,0:T(8,128)(2,1)S(1)}, bf16[2,80,8,128]{3,2,1,0:T(8,128)(2,1)S(1)}, u32[]{:S(2)}, u32[]{:S(2)}) collective-permute-start(bf16[2,80,8,128]{3,2,1,0:T(8,128)(2,1)S(1)} %get-tuple-element.16), channel_id=1, source_target_pairs={{0,1},{1,2},{2,3},{4,5},{5,6},{6,7},{8,9},{9,10},{10,11},{12,13},{... | collective-permute-start | bytes 983048 | tf_op jit(solution)/shard_map/ppermute | solution.py:29
  28.6 1.3 collective-permute-start.3
  29.9 3.3 %broadcast_multiply_fusion = (bf16[80,80,128]{2,1,0:T(8,128)(2,1)}, bf16[80,80,128]{2,1,0:T(8,128)(2,1)}) fusion(bf16[80,80]{1,0:T(8,128)(2,1)S(1)} %get-tuple-element.22, bf16[128]{0:T(256)(128)(2,1)S(1)} %fusion.2, bf16[80,80]{1,0:T(8,128)(2,1)S(1)} %get-tuple-element.23), kind=kLoop, calls=%fused_computation.8 | loop fusion | flops 1638400 | bytes 3302656 | tf_op jit(solution)/shard_map/mul | solution.py:152
  33.3 1.2 collective-permute-done.2
  34.5 3.9 %collective-permute-done.3 = bf16[2,80,8,128]{3,2,1,0:T(8,128)(2,1)S(1)} collective-permute-done((bf16[2,80,8,128]{3,2,1,0:T(8,128)(2,1)S(1)}, bf16[2,80,8,128]{3,2,1,0:T(8,128)(2,1)S(1)}, u32[]{:S(2)}, u32[]{:S(2)}) %collective-permute-start.3) | collective-permute-done | bytes 327712 | tf_op jit(solution)/shard_map/ppermute | solution.py:31
  38.3 2.2 %pad_maximum_fusion = bf16[2,80,80,128]{3,2,1,0:T(8,128)(2,1)S(1)} fusion(bf16[2,80,8,128]{3,2,1,0:T(8,128)(2,1)S(1)} %collective-permute-done.3, bf16[2,8,64,128]{3,2,1,0:T(8,128)(2,1)S(1)} %collective-permute-done.1, bf16[1,64,64,128]{3,2,1,0:T(8,128)(2,1)S(1)} %get-tuple-element.30, bf16[1,64,64,128]{3,2,1,0:T(8,128)(2,1)S(1)} %get-tuple-element.31, ...), kind=kLoop, calls=%fused_computation | loop fusion | flops 19660800 | bytes 6553600 | tf_op jit(solution)/shard_map/concatenate | solution.py:27
  40.5 2.3 %slice_bitcast_fusion.2 = (bf16[80,80,128]{2,1,0:T(8,128)(2,1)}, bf16[80,80,128]{2,1,0:T(8,128)(2,1)}) fusion(bf16[2,80,80,128]{3,2,1,0:T(8,128)(2,1)S(1)} %pad_maximum_fusion), kind=kLoop, calls=%fused_computation.4 | loop fusion | bytes 6553600 | tf_op jit(solution)/shard_map/squeeze | solution.py:148
  42.8 1.6 mul.17.mask_b
  44.4 1.6 mul.16.mask_a
  46.0 59.0 %shard_map.113 = (f32[64,64,128]{2,1,0:T(8,128)}, f32[64,64,128]{2,1,0:T(8,128)}, bf16[64,64,128]{2,1,0:T(8,128)(2,1)}, bf16[64,64,128]{2,1,0:T(8,128)(2,1)}) custom-call(f32[64,64,128]{2,1,0:T(8,128)} %feat_a.1, f32[64,64,128]{2,1,0:T(8,128)} %feat_b.1, bf16[64,64,128]{2,1,0:T(8,128)(2,1)} %mul.16.mask_a, bf16[64,64,128]{2,1,0:T(8,128)(2,1)} %mul.17.mask_b, ...), custom_call_target="tpu_custom_call" | custom-call | tf_op jit(solution)/shard_map/pallas_call | solution.py:136
  105.0 0.0 copy-start
  105.0 0.0 copy-start.1
  105.0 1.3 pad_maximum_fusion.11
  106.3 5.5 %collective-permute-start.8 = (bf16[2,8,64,128]{3,2,1,0:T(8,128)(2,1)S(1)}, bf16[2,8,64,128]{3,2,1,0:T(8,128)(2,1)S(1)}, u32[]{:S(2)}, u32[]{:S(2)}) collective-permute-start(bf16[2,8,64,128]{3,2,1,0:T(8,128)(2,1)S(1)} %get-tuple-element.18), channel_id=1, source_target_pairs={{0,4},{4,8},{8,12},{12,16},{16,20},{20,24},{24,28},{1,5},{5,9},{9,... | collective-permute-start | bytes 786440 | tf_op jit(solution)/shard_map/ppermute | solution.py:29
  111.8 1.9 collective-permute-start.9
  113.7 1.6 collective-permute-done.8
  115.3 5.0 %collective-permute-done.9 = bf16[2,8,64,128]{3,2,1,0:T(8,128)(2,1)S(1)} collective-permute-done((bf16[2,8,64,128]{3,2,1,0:T(8,128)(2,1)S(1)}, bf16[2,8,64,128]{3,2,1,0:T(8,128)(2,1)S(1)}, u32[]{:S(2)}, u32[]{:S(2)}) %collective-permute-start.9) | collective-permute-done | bytes 262176 | tf_op jit(solution)/shard_map/ppermute | solution.py:31
  120.4 0.0 copy-done
  120.4 0.0 copy-done.1
  120.4 0.1 pad_maximum_fusion.5
  120.5 3.2 %collective-permute-start.10 = (bf16[2,80,8,128]{3,2,1,0:T(8,128)(2,1)S(1)}, bf16[2,80,8,128]{3,2,1,0:T(8,128)(2,1)S(1)}, u32[]{:S(2)}, u32[]{:S(2)}) collective-permute-start(bf16[2,80,8,128]{3,2,1,0:T(8,128)(2,1)S(1)} %get-tuple-element.14), channel_id=1, source_target_pairs={{0,1},{1,2},{2,3},{4,5},{5,6},{6,7},{8,9},{9,10},{10,11},{12,13},{... | collective-permute-start | bytes 983048 | tf_op jit(solution)/shard_map/ppermute | solution.py:29
  123.7 1.3 collective-permute-start.11
  125.0 4.6 %collective-permute-done.10 = bf16[2,80,8,128]{3,2,1,0:T(8,128)(2,1)S(1)} collective-permute-done((bf16[2,80,8,128]{3,2,1,0:T(8,128)(2,1)S(1)}, bf16[2,80,8,128]{3,2,1,0:T(8,128)(2,1)S(1)}, u32[]{:S(2)}, u32[]{:S(2)}) %collective-permute-start.10) | collective-permute-done | bytes 327712 | tf_op jit(solution)/shard_map/ppermute | solution.py:29
  129.6 4.1 %collective-permute-done.11 = bf16[2,80,8,128]{3,2,1,0:T(8,128)(2,1)S(1)} collective-permute-done((bf16[2,80,8,128]{3,2,1,0:T(8,128)(2,1)S(1)}, bf16[2,80,8,128]{3,2,1,0:T(8,128)(2,1)S(1)}, u32[]{:S(2)}, u32[]{:S(2)}) %collective-permute-start.11) | collective-permute-done | bytes 327712 | tf_op jit(solution)/shard_map/ppermute | solution.py:31
  133.7 2.2 %pad_maximum_fusion.1 = bf16[2,80,80,128]{3,2,1,0:T(8,128)(2,1)S(1)} fusion(bf16[2,80,8,128]{3,2,1,0:T(8,128)(2,1)S(1)} %collective-permute-done.11, bf16[2,8,64,128]{3,2,1,0:T(8,128)(2,1)S(1)} %collective-permute-done.9, bf16[1,64,64,128]{3,2,1,0:T(8,128)(2,1)S(1)} %bitcast.27, bf16[1,64,64,128]{3,2,1,0:T(8,128)(2,1)S(1)} %bitcast.24, ...), kind=kLoop, calls=%fused_computation.1 | loop fusion | flops 19660800 | bytes 6553600 | tf_op jit(solution)/shard_map/concatenate | solution.py:27
  135.9 2.4 %slice_bitcast_fusion = (bf16[80,80,128]{2,1,0:T(8,128)(2,1)}, bf16[80,80,128]{2,1,0:T(8,128)(2,1)}) fusion(bf16[2,80,80,128]{3,2,1,0:T(8,128)(2,1)S(1)} %pad_maximum_fusion.1), kind=kLoop, calls=%fused_computation.2 | loop fusion | bytes 6553600 | tf_op jit(solution)/shard_map/squeeze | solution.py:148
  138.3 58.8 %shard_map.114 = (f32[64,64,128]{2,1,0:T(8,128)}, f32[64,64,128]{2,1,0:T(8,128)}) custom-call(f32[64,64,128]{2,1,0:T(8,128)} %get-tuple-element.6.feat_a, f32[64,64,128]{2,1,0:T(8,128)} %get-tuple-element.7.feat_b, bf16[64,64,128]{2,1,0:T(8,128)(2,1)} %mul.16.mask_a, bf16[64,64,128]{2,1,0:T(8,128)(2,1)} %mul.17.mask_b, ...), custom_call_target="tpu_custom_call" | custom-call | tf_op jit(solution)/shard_map/pallas_call | solution.py:136
  (7 shorter events, 0.1 us)
Async XLA Ops:
  2.2 14.9 %collective-permute-start.4 = (bf16[2,8,64]{2,1,0:T(8,128)(2,1)S(1)}, bf16[2,8,64]{2,1,0:T(8,128)(2,1)S(1)}, u32[]{:S(2)}, u32[]{:S(2)}) collective-permute-start(bf16[2,8,64]{2,1,0:T(8,128)(2,1)S(1)} %get-tuple-element.26), channel_id=1, source_target_pairs={{0,4},{4,8},{8,12},{12,16},{16,20},{20,24},{24,28},{1,5},{5,9},{9,... | collective-permute-start | bytes 6152 | tf_op jit(solution)/shard_map/ppermute | solution.py:29
  5.9 15.9 %copy-start.2 = (s32[64,64]{1,0:T(8,128)S(1)}, s32[64,64]{1,0:T(8,128)}, u32[]{:S(2)}) copy-start(s32[64,64]{1,0:T(8,128)} %param.12) | copy-start | bytes 49156
  5.9 15.9 %copy-start.3 = (s32[64,64]{1,0:T(8,128)S(1)}, s32[64,64]{1,0:T(8,128)}, u32[]{:S(2)}) copy-start(s32[64,64]{1,0:T(8,128)} %param.13) | copy-start | bytes 49156
  5.9 11.2 %collective-permute-start.5 = (bf16[2,8,64]{2,1,0:T(8,128)(2,1)S(1)}, bf16[2,8,64]{2,1,0:T(8,128)(2,1)S(1)}, u32[]{:S(2)}, u32[]{:S(2)}) collective-permute-start(bf16[2,8,64]{2,1,0:T(8,128)(2,1)S(1)} %get-tuple-element.27), channel_id=1, source_target_pairs={{4,0},{8,4},{12,8},{16,12},{20,16},{24,20},{28,24},{5,1},{9,5},{13... | collective-permute-start | bytes 6152 | tf_op jit(solution)/shard_map/ppermute | solution.py:31
  10.6 14.7 %collective-permute-start = (bf16[2,8,64,128]{3,2,1,0:T(8,128)(2,1)S(1)}, bf16[2,8,64,128]{3,2,1,0:T(8,128)(2,1)S(1)}, u32[]{:S(2)}, u32[]{:S(2)}) collective-permute-start(bf16[2,8,64,128]{3,2,1,0:T(8,128)(2,1)S(1)} %get-tuple-element.20), channel_id=1, source_target_pairs={{0,4},{4,8},{8,12},{12,16},{16,20},{20,24},{24,28},{1,5},{5,9},{9,... | collective-permute-start | bytes 786440 | tf_op jit(solution)/shard_map/ppermute | solution.py:29
  15.1 10.1 %collective-permute-start.1 = (bf16[2,8,64,128]{3,2,1,0:T(8,128)(2,1)S(1)}, bf16[2,8,64,128]{3,2,1,0:T(8,128)(2,1)S(1)}, u32[]{:S(2)}, u32[]{:S(2)}) collective-permute-start(bf16[2,8,64,128]{3,2,1,0:T(8,128)(2,1)S(1)} %get-tuple-element.21), channel_id=1, source_target_pairs={{4,0},{8,4},{12,8},{16,12},{20,16},{24,20},{28,24},{5,1},{9,5},{13... | collective-permute-start | bytes 786440 | tf_op jit(solution)/shard_map/ppermute | solution.py:31
  17.2 4.6 %collective-permute-start.6 = (bf16[2,80,8]{2,1,0:T(8,128)(2,1)S(1)}, bf16[2,80,8]{2,1,0:T(8,128)(2,1)S(1)}, u32[]{:S(2)}, u32[]{:S(2)}) collective-permute-start(bf16[2,80,8]{2,1,0:T(8,128)(2,1)S(1)} %get-tuple-element.24), channel_id=1, source_target_pairs={{0,1},{1,2},{2,3},{4,5},{5,6},{6,7},{8,9},{9,10},{10,11},{12,13},{... | collective-permute-start | bytes 7688 | tf_op jit(solution)/shard_map/ppermute | solution.py:29
  20.4 4.7 %collective-permute-start.7 = (bf16[2,80,8]{2,1,0:T(8,128)(2,1)S(1)}, bf16[2,80,8]{2,1,0:T(8,128)(2,1)S(1)}, u32[]{:S(2)}, u32[]{:S(2)}) collective-permute-start(bf16[2,80,8]{2,1,0:T(8,128)(2,1)S(1)} %get-tuple-element.25), channel_id=1, source_target_pairs={{1,0},{2,1},{3,2},{5,4},{6,5},{7,6},{9,8},{10,9},{11,10},{13,12},{... | collective-permute-start | bytes 7688 | tf_op jit(solution)/shard_map/ppermute | solution.py:31
  25.4 9.1 %collective-permute-start.2 = (bf16[2,80,8,128]{3,2,1,0:T(8,128)(2,1)S(1)}, bf16[2,80,8,128]{3,2,1,0:T(8,128)(2,1)S(1)}, u32[]{:S(2)}, u32[]{:S(2)}) collective-permute-start(bf16[2,80,8,128]{3,2,1,0:T(8,128)(2,1)S(1)} %get-tuple-element.16), channel_id=1, source_target_pairs={{0,1},{1,2},{2,3},{4,5},{5,6},{6,7},{8,9},{9,10},{10,11},{12,13},{... | collective-permute-start | bytes 983048 | tf_op jit(solution)/shard_map/ppermute | solution.py:29
  28.6 9.7 %collective-permute-start.3 = (bf16[2,80,8,128]{3,2,1,0:T(8,128)(2,1)S(1)}, bf16[2,80,8,128]{3,2,1,0:T(8,128)(2,1)S(1)}, u32[]{:S(2)}, u32[]{:S(2)}) collective-permute-start(bf16[2,80,8,128]{3,2,1,0:T(8,128)(2,1)S(1)} %get-tuple-element.17), channel_id=1, source_target_pairs={{1,0},{2,1},{3,2},{5,4},{6,5},{7,6},{9,8},{10,9},{11,10},{13,12},{... | collective-permute-start | bytes 983048 | tf_op jit(solution)/shard_map/ppermute | solution.py:31
  105.0 15.4 %copy-start = (bf16[64,64,128]{2,1,0:T(8,128)(2,1)S(1)}, bf16[64,64,128]{2,1,0:T(8,128)(2,1)}, u32[]{:S(2)}) copy-start(bf16[64,64,128]{2,1,0:T(8,128)(2,1)} %get-tuple-element.8) | copy-start | bytes 3145732
  105.0 15.4 %copy-start.1 = (bf16[64,64,128]{2,1,0:T(8,128)(2,1)S(1)}, bf16[64,64,128]{2,1,0:T(8,128)(2,1)}, u32[]{:S(2)}) copy-start(bf16[64,64,128]{2,1,0:T(8,128)(2,1)} %get-tuple-element.9) | copy-start | bytes 3145732
  106.3 9.1 %collective-permute-start.8 = (bf16[2,8,64,128]{3,2,1,0:T(8,128)(2,1)S(1)}, bf16[2,8,64,128]{3,2,1,0:T(8,128)(2,1)S(1)}, u32[]{:S(2)}, u32[]{:S(2)}) collective-permute-start(bf16[2,8,64,128]{3,2,1,0:T(8,128)(2,1)S(1)} %get-tuple-element.18), channel_id=1, source_target_pairs={{0,4},{4,8},{8,12},{12,16},{16,20},{20,24},{24,28},{1,5},{5,9},{9,... | collective-permute-start | bytes 786440 | tf_op jit(solution)/shard_map/ppermute | solution.py:29
  111.8 8.6 %collective-permute-start.9 = (bf16[2,8,64,128]{3,2,1,0:T(8,128)(2,1)S(1)}, bf16[2,8,64,128]{3,2,1,0:T(8,128)(2,1)S(1)}, u32[]{:S(2)}, u32[]{:S(2)}) collective-permute-start(bf16[2,8,64,128]{3,2,1,0:T(8,128)(2,1)S(1)} %get-tuple-element.19), channel_id=1, source_target_pairs={{4,0},{8,4},{12,8},{16,12},{20,16},{24,20},{28,24},{5,1},{9,5},{13... | collective-permute-start | bytes 786440 | tf_op jit(solution)/shard_map/ppermute | solution.py:31
  120.5 9.1 %collective-permute-start.10 = (bf16[2,80,8,128]{3,2,1,0:T(8,128)(2,1)S(1)}, bf16[2,80,8,128]{3,2,1,0:T(8,128)(2,1)S(1)}, u32[]{:S(2)}, u32[]{:S(2)}) collective-permute-start(bf16[2,80,8,128]{3,2,1,0:T(8,128)(2,1)S(1)} %get-tuple-element.14), channel_id=1, source_target_pairs={{0,1},{1,2},{2,3},{4,5},{5,6},{6,7},{8,9},{9,10},{10,11},{12,13},{... | collective-permute-start | bytes 983048 | tf_op jit(solution)/shard_map/ppermute | solution.py:29
  123.7 10.0 %collective-permute-start.11 = (bf16[2,80,8,128]{3,2,1,0:T(8,128)(2,1)S(1)}, bf16[2,80,8,128]{3,2,1,0:T(8,128)(2,1)S(1)}, u32[]{:S(2)}, u32[]{:S(2)}) collective-permute-start(bf16[2,80,8,128]{3,2,1,0:T(8,128)(2,1)S(1)} %get-tuple-element.15), channel_id=1, source_target_pairs={{1,0},{2,1},{3,2},{5,4},{6,5},{7,6},{9,8},{10,9},{11,10},{13,12},{... | collective-permute-start | bytes 983048 | tf_op jit(solution)/shard_map/ppermute | solution.py:31
where the time goes:
time: 198 us; the launch traced here: 197 us
  Pallas kernels  118 us (60%)
  starting transfers between devices  33 us (17%)
  waiting for transfers between devices  23.8 us (12%)
  other arithmetic  13.7 us (7%)
  local copies, waits for them, and re-layouts  7.92 us (4%)
    pallas_call x2, Pallas kernels, one_pass(): pl.pallas_call(pass_kernel, grid=(rows // band,), in_specs=[strip] * 4 +...  118 us
    ppermute x6, starting transfers between devices, extended(): lax.ppermute(tail, axis, [(i, (i + 1) % count) for i in range(ends)])  23.3 us
    ppermute x6, waiting for transfers between devices, extended(): lax.ppermute(head, axis, [((i + 1) % count, i) for i in range(ends)])  16.4 us
    ppermute x6, starting transfers between devices, extended(): lax.ppermute(head, axis, [((i + 1) % count, i) for i in range(ends)])  9.64 us
    ppermute x6, waiting for transfers between devices, extended(): lax.ppermute(tail, axis, [(i, (i + 1) % count) for i in range(ends)])  7.4 us
    squeeze x2, local copies, waits for them, and re-layouts, halo(): return (both[0], both[1])  4.63 us
    concatenate x4, other arithmetic, extended(): jnp.concatenate([lax.ppermute(tail, axis, [(i, (i + 1) % count) for i in...  4.48 us
    another operation x3, other arithmetic, halo(): both = extended(jnp.stack([half_a, half_b]), (('gy', 1), ('gx', 2)), R)  4.25 us
  transfers between devices with their start and end apart: 12, of which 7 were waited for; matrix products, arithmetic and copies ran while one was open for 3% of the time, Pallas kernels for 0%

commit v1 on v0

v1 whole, which is shorter than its diff:
```python
import functools

import jax
import jax.numpy as jnp
import numpy as np
from jax import lax
from jax.experimental import pallas as pl
from jax.experimental.pallas import tpu as pltpu
from jax.sharding import PartitionSpec as P

R = 8
band = 8
tile_width = 16
key_rows = band + 2 * R
key_width = tile_width + 2 * R
chunk = band * key_width
BLOCKED = -1e30
COL_LANE = 3 * band
EMPTY_LANE = COL_LANE + 2 * tile_width
ONE_LANE = EMPTY_LANE + 1
EMPTY = 2.0**20


def halo_kernel(half_a, half_b, ext_a, ext_b, send_sems, recv_sems, *, axes):
    rows, cols, channels = half_a.shape
    me = [lax.axis_index(axis) for axis in axes]
    counts = [lax.axis_size(axis) for axis in axes]
    ways = [(dy, dx) for dy in (-1, 0, 1) for dx in (-1, 0, 1) if (dy, dx) != (0, 0)]

    def present(way):
        there = [m + d for m, d in zip(me, way)]
        ok = None
        for t, d, n in zip(there, way, counts):
            if d:
                test = (t >= 0) if d < 0 else (t < n)
                ok = test if ok is None else jnp.logical_and(ok, test)
        return ok

    def edge(d, size):
        return {-1: (0, R), 0: (0, size), 1: (size - R, R)}[d]

    def landing(d, size):
        return {-1: (R + size, R), 0: (R, size), 1: (0, R)}[d]

    def copy(i, way, survey):
        y, x = edge(way[0], rows), edge(way[1], cols)
        to_y, to_x = landing(way[0], rows), landing(way[1], cols)
        half, ext = ((half_a, ext_a), (half_b, ext_b))[survey]
        return pltpu.make_async_remote_copy(
            src_ref=half.at[pl.ds(*y), pl.ds(*x)],
            dst_ref=ext.at[pl.ds(*to_y), pl.ds(*to_x)],
            send_sem=send_sems.at[survey, i],
            recv_sem=recv_sems.at[survey, i],
            device_id=(me[0] + way[0], me[1] + way[1]),
            device_id_type=pl.DeviceIdType.MESH,
        )

    barrier = pltpu.get_barrier_semaphore()
    for way in ways:

        @pl.when(present(way))
        def _(way=way):
            pl.semaphore_signal(
                barrier,
                inc=1,
                device_id=(me[0] + way[0], me[1] + way[1]),
                device_id_type=pl.DeviceIdType.MESH,
            )

    near = [jnp.where(m > 0, 2, 1) + jnp.where(m < n - 1, 1, 0) for m, n in zip(me, counts)]
    pl.semaphore_wait(barrier, near[0] * near[1] - 1)

    for i, way in enumerate(ways):

        @pl.when(present(way))
        def _(i=i, way=way):
            copy(i, way, 0).start()
            copy(i, way, 1).start()

    def move(row, carry):
        for half, ext in ((half_a, ext_a), (half_b, ext_b)):
            ext[R + row, pl.ds(R, cols), :] = half[row]
        return carry

    lax.fori_loop(0, rows, move, 0)

    for i, way in enumerate(ways):
        source = (-way[0], -way[1])

        @pl.when(present(way))
        def _(i=i, way=way):
            copy(i, way, 0).wait_send()
            copy(i, way, 1).wait_send()

        @pl.when(present(source))
        def _(i=i, way=way):
            copy(i, way, 0).wait_recv()
            copy(i, way, 1).wait_recv()

        @pl.when(jnp.logical_not(present(source)))
        def _(way=way):
            (y, height), (x, width) = landing(way[0], rows), landing(way[1], cols)

            def fill(row, carry):
                for ext in (ext_a, ext_b):
                    ext[row, pl.ds(x, width), :] = jnp.full((width, channels), EMPTY, ext.dtype)
                return carry

            lax.fori_loop(y, y + height, fill, 0)


def halo(half_a, half_b, index):
    rows, cols, channels = half_a.shape
    ext = jax.ShapeDtypeStruct((rows + 2 * R, cols + 2 * R, channels), half_a.dtype)
    return pl.pallas_call(
        functools.partial(halo_kernel, axes=("gy", "gx")),
        out_shape=[ext] * 2,
        in_specs=[pl.BlockSpec(memory_space=pltpu.VMEM)] * 2,
        out_specs=[pl.BlockSpec(memory_space=pltpu.VMEM)] * 2,
        scratch_shapes=[pltpu.SemaphoreType.DMA((2, 8)), pltpu.SemaphoreType.DMA((2, 8))],
        compiler_params=pltpu.CompilerParams(collective_id=index, has_side_effects=True),
    )(half_a, half_b)


def query_kinds(channels):
    lanes = np.zeros((3, 2, band, tile_width, channels), np.float32)
    for kind in range(3):
        for i in range(band):
            lanes[kind, :, i, :, kind * band + i] = 1.0
    for kind in range(2):
        for i in range(tile_width):
            lanes[:, kind, :, i, COL_LANE + kind * tile_width + i] = 1.0
    lanes[..., EMPTY_LANE] = 1.0
    return jnp.asarray(lanes.reshape(6, band * tile_width, channels), jnp.bfloat16)


def key_pattern(cols, channels):
    y = np.arange(3 * band)[:, None, None]
    x = np.arange(cols)[None, :, None]
    lane = np.arange(channels)[None, None, :]
    part = (y // band - lane // band) % 3
    row, want_row = y % band, lane % band
    row_out = (lane < COL_LANE) & (((part == 0) & (row < want_row)) | ((part == 2) & (row > want_row)))
    col_lane = lane - COL_LANE
    first = (x // tile_width) % 2 == col_lane // tile_width
    col, want_col = x % tile_width, col_lane % tile_width
    col_out = (
        (lane >= COL_LANE)
        & (lane < EMPTY_LANE)
        & ((first & (col < want_col)) | (~first & (col > want_col)))
    )
    one = np.where(lane == ONE_LANE, 1.0, 0.0)
    return jnp.asarray(np.where(row_out | col_out, BLOCKED, one), jnp.bfloat16)


def gelu(x):
    return x * (0.5 * lax.erf(x * 0.5**0.5) + 0.5)


def pass_kernel(
    feat_a, feat_b, keys_a, keys_b, pattern, kinds, first, second, *refs, halves
):
    outs = refs[: 4 if halves else 2]
    lanes_a, lanes_b, scores_a, scores_b, peak_a, peak_b, joined_a, joined_b = refs[len(outs) :]
    strip, cols, channels = feat_a.shape
    across = cols // tile_width
    count = (strip // band) * across
    rate = 1.0 / (channels**0.5 * np.log(2.0))
    feats, keys, lanes = (feat_a, feat_b), (keys_b, keys_a), (lanes_b, lanes_a)
    own = (keys_a, keys_b)
    scores, peaks, joins = (scores_a, scores_b), (peak_a, peak_b), (joined_a, joined_b)
    step_index = pl.program_id(0)

    @pl.when(step_index == 0)
    def _():
        lane = lax.broadcasted_iota(jnp.int32, (keys_a.shape[1], channels), 1)
        empty = jnp.where(lane == EMPTY_LANE, BLOCKED, 0.0).astype(jnp.bfloat16)
        zero = jnp.zeros_like(empty)

        def fill(row, carry):
            base = pattern[row % (3 * band)]
            for key, lane_ref in ((keys_a, lanes_a), (keys_b, lanes_b)):
                lane_ref[row] = base + jnp.where(key[row] >= EMPTY, empty, zero)
            return carry

        lax.fori_loop(0, keys_a.shape[0], fill, 0)

    def place(tile):
        tile = jnp.clip(tile, 0, count - 1)
        down, side = tile // across, tile % across
        inside = pl.multiple_of(down * band, band)
        top = pl.multiple_of(step_index * strip + inside, band)
        return inside, top, pl.multiple_of(side * tile_width, tile_width)

    def cells(s, tile):
        inside, _, left = place(tile)
        return feats[s][pl.ds(inside, band), pl.ds(left, tile_width), :].reshape(-1, channels)

    def wide(s, tile, part):
        _, top, left = place(tile)
        at = (pl.ds(pl.multiple_of(top + part * band, band), band), pl.ds(left, key_width))
        return jnp.concatenate(
            [keys[s][at].reshape(-1, channels), lanes[s][at].reshape(-1, channels)], axis=1
        )

    def half_step(s_new, tile_new, s_old, tile_old, s_mlp, tile_mlp):
        _, top, left = place(tile_new)
        kind = ((top // band) % 3) * 2 + (left // tile_width) % 2
        queries = jnp.concatenate([cells(s_new, tile_new).astype(jnp.bfloat16), kinds[kind]], axis=1)
        old_peak = peaks[s_old][...]
        old_top = jnp.concatenate([old_peak, old_peak], axis=1)
        best = None
        total = None
        hidden_in = jnp.dot(joins[s_mlp][...], first[...], preferred_element_type=jnp.float32)
        for part in range(3):
            got = lax.dot_general(
                queries,
                wide(s_new, tile_new, part),
                (((1,), (1,)), ((), ())),
                preferred_element_type=jnp.float32,
            )
            weight = jnp.exp2((scores[s_old][part] - old_top) * rate).astype(jnp.bfloat16)
            term = jnp.dot(weight, wide(s_old, tile_old, part), preferred_element_type=jnp.float32)
            total = term if part == 0 else total + term
            scores[s_new][part] = got
            high = jnp.maximum(got[:, :channels], got[:, channels:])
            best = high if part == 0 else jnp.maximum(best, high)
            if part == 0:
                hidden = gelu(hidden_in).astype(jnp.bfloat16)
            if part == 1:
                update = jnp.dot(hidden, second[...], preferred_element_type=jnp.float32)
        peaks[s_new][...] = jnp.broadcast_to(
            jnp.maximum(jnp.max(best, axis=1, keepdims=True), 0.0), best.shape
        )
        mass = channels + ONE_LANE
        denominator = jnp.exp2(-old_peak * rate) + total[:, mass : mass + 1]
        carried = total[:, :channels] / denominator
        inside, top, left = place(tile_mlp)
        held = own[s_mlp][pl.ds(pl.multiple_of(top + R, R), band), pl.ds(pl.multiple_of(left + R, R), tile_width), :]
        held = held.reshape(-1, channels).astype(jnp.float32) < EMPTY
        new = cells(s_mlp, tile_mlp) + jnp.where(held, update, 0.0)
        sent = jnp.where(held, new, EMPTY).reshape(band, tile_width, channels)
        new = new.reshape(band, tile_width, channels)
        at = (pl.ds(inside, band), pl.ds(left, tile_width))
        outs[s_mlp][at] = new
        if halves:
            outs[s_mlp + 2][at] = sent.astype(jnp.bfloat16)
        joins[s_old][:, :channels] = cells(s_old, tile_old).astype(jnp.bfloat16)
        joins[s_old][:, channels:] = carried.astype(jnp.bfloat16)

    def step(tile, carry):
        half_step(0, tile, 1, tile - 1, 0, tile - 1)
        half_step(1, tile, 0, tile, 1, tile - 1)
        return carry

    lax.fori_loop(0, count + 1, step, 0)


def one_pass(feats, keys, weights, halves):
    rows, cols, channels = feats[0].shape
    height = 2 * band if rows % (2 * band) == 0 else band
    strip = pl.BlockSpec((height, cols, channels), lambda i: (i, 0, 0))
    cells = band * tile_width

    def whole(x):
        return pl.BlockSpec(x.shape, lambda i: (0,) * x.ndim)

    rest = (*keys, key_pattern(keys[0].shape[1], channels), query_kinds(channels), *weights)
    out_shape = [jax.ShapeDtypeStruct(feats[0].shape, jnp.float32)] * 2
    if halves:
        out_shape += [jax.ShapeDtypeStruct(feats[0].shape, jnp.bfloat16)] * 2
    return pl.pallas_call(
        functools.partial(pass_kernel, halves=halves),
        grid=(rows // height,),
        in_specs=[strip] * 2 + [whole(x) for x in rest],
        out_specs=[strip] * len(out_shape),
        out_shape=out_shape,
        scratch_shapes=[pltpu.VMEM(keys[0].shape, jnp.bfloat16)] * 2
        + [pltpu.VMEM((3, cells, chunk), jnp.float32)] * 2
        + [pltpu.VMEM((cells, channels), jnp.float32)] * 2
        + [pltpu.VMEM((cells, 2 * channels), jnp.bfloat16)] * 2,
        compiler_params=pltpu.CompilerParams(vmem_limit_bytes=56 * 2**20),
    )(*feats, *rest)


def keyed(feat, occ):
    return jnp.where(occ[..., None] > 0, feat, EMPTY).astype(jnp.bfloat16)


def local(feat_a, feat_b, occ_a, occ_b, first_weight, second_weight):
    weights = (first_weight, second_weight)
    keys = halo(keyed(feat_a, occ_a), keyed(feat_b, occ_b), 0)
    new_a, new_b, half_a, half_b = one_pass((feat_a, feat_b), keys, weights, True)
    keys = halo(half_a, half_b, 1)
    return tuple(one_pass((new_a, new_b), keys, weights, False))


def solution(mesh):
    in_specs = (P("gy", "gx", None), P("gy", "gx", None), P("gy", "gx"), P("gy", "gx"), P(), P())
    out_specs = (P("gy", "gx", None), P("gy", "gx", None))
    return jax.shard_map(local, mesh=mesh, in_specs=in_specs, out_specs=out_specs, check_vma=False)
```

time: 198 us -> 110 us (0.56)
  starting transfers between devices: 33 us -> 0 us
  waiting for transfers between devices: 23.8 us -> 0 us
  Pallas kernels: 118 us -> 102 us
  local copies, waits for them, and re-layouts: 7.92 us -> 0 us
  other arithmetic: 13.7 us -> 6.27 us
    ppermute x12 -> x0, starting transfers between devices: 33 us -> none  [the longest x6 23.3 us: extended(): lax.ppermute(tail, axis, [(i, (i + 1) % count) for i in range(ends)])]
    ppermute x12 -> x0, waiting for transfers between devices: 23.8 us -> none  [the longest x6 16.4 us: extended(): lax.ppermute(head, axis, [((i + 1) % count, i) for i in range(ends)])]
    pallas_call x2 -> x4, Pallas kernels: 118 us -> 102 us  [the longest x2 71.8 us: one_pass(): pl.pallas_call(functools.partial(pass_kernel, halves=halves), grid=(rows...]
    convert_element_type x3 -> x1, other arithmetic: 0.02 us -> 4.74 us  [keyed(): return jnp.where(occ[..., None] > 0, feat, EMPTY).astype(jnp.bfloat16)]
    squeeze x2 -> x0, local copies, waits for them, and re-layouts: 4.63 us -> none  [halo(): return (both[0], both[1])]
    concatenate x4 -> x0, other arithmetic: 4.48 us -> none  [extended(): jnp.concatenate([lax.ppermute(tail, axis, [(i, (i + 1) % count) for i in...]
    another operation x3 -> x0, other arithmetic: 4.25 us -> none  [halo(): both = extended(jnp.stack([half_a, half_b]), (('gy', 1), ('gx', 2)), R)]
    mul x1 -> x0, other arithmetic: 3.34 us -> none  [spread(): return (mask[..., None] * lane_values).astype(jnp.bfloat16)]
  transfers between devices with their start and end apart: 12 -> 0, of which waited for: 7 -> 0; matrix products, arithmetic and copies ran while one was open for 3% -> 0% of each run, Pallas kernels for 0% -> 0%
where the time goes in v1:
time: 110 us; the launch traced here: 109 us
  Pallas kernels  102 us (93%)
  other arithmetic  6.27 us (6%)
    pallas_call x2, Pallas kernels, one_pass(): pl.pallas_call(functools.partial(pass_kernel, halves=halves), grid=(rows...  71.8 us
    pallas_call x2, Pallas kernels, halo(): pl.pallas_call(functools.partial(halo_kernel, axes=('gy', 'gx')), out_sha...  30.5 us
    convert_element_type x1, other arithmetic, keyed(): return jnp.where(occ[..., None] > 0, feat, EMPTY).astype(jnp.bfloat16)  4.74 us

profile of v1, /device:TPU:3, one launch (start us, length us, event | category | flops | bytes accessed | tf_op | source)
XLA Modules:
  0.0 109.2 jit_solution(12854909866219270676)
XLA Ops:
  0.6 0.8 broadcast_compare_fusion.1
  1.4 0.8 broadcast_compare_fusion
  2.2 4.7 %select_convert_fusion = (bf16[64,64,128]{2,1,0:T(8,128)(2,1)}, bf16[64,64,128]{2,1,0:T(8,128)(2,1)}) fusion(f32[64,64,128]{2,1,0:T(8,128)} %feat_b.1, pred[64,64]{1,0:T(8,128)(4,1)S(1)} %broadcast_compare_fusion, f32[64,64,128]{2,1,0:T(8,128)} %feat_a.1, pred[64,64]{1,0:T(8,128)(4,1)S(1)} %broadcast_compare_fusion.1), kind=kLoop, calls=%fused_computation | loop fusion | flops 1048576 | bytes 6299648 | tf_op jit(solution)/shard_map/convert_element_type | solution.py:287
  6.9 15.5 %shard_map.113 = (bf16[80,80,128]{2,1,0:T(8,128)(2,1)}, bf16[80,80,128]{2,1,0:T(8,128)(2,1)}) custom-call(bf16[64,64,128]{2,1,0:T(8,128)(2,1)} %get-tuple-element.19.half_a, bf16[64,64,128]{2,1,0:T(8,128)(2,1)} %get-tuple-element.18.half_b), custom_call_target="tpu_custom_call" | custom-call | tf_op jit(solution)/shard_map/pallas_call | solution.py:115
  22.4 36.0 %shard_map.114 = (f32[64,64,128]{2,1,0:T(8,128)}, f32[64,64,128]{2,1,0:T(8,128)}, bf16[64,64,128]{2,1,0:T(8,128)(2,1)}, bf16[64,64,128]{2,1,0:T(8,128)(2,1)}) custom-call(f32[64,64,128]{2,1,0:T(8,128)} %feat_a.1, f32[64,64,128]{2,1,0:T(8,128)} %feat_b.1, bf16[80,80,128]{2,1,0:T(8,128)(2,1)} %get-tuple-element.10.keys_a, ...), custom_call_target="tpu_custom_call" | custom-call | tf_op jit(solution)/shard_map/pallas_call | solution.py:272
  58.4 15.0 %shard_map.115 = (bf16[80,80,128]{2,1,0:T(8,128)(2,1)}, bf16[80,80,128]{2,1,0:T(8,128)(2,1)}) custom-call(bf16[64,64,128]{2,1,0:T(8,128)(2,1)} %get-tuple-element.14.half_a, bf16[64,64,128]{2,1,0:T(8,128)(2,1)} %get-tuple-element.15.half_b), custom_call_target="tpu_custom_call" | custom-call | tf_op jit(solution)/shard_map/pallas_call | solution.py:115
  73.4 35.8 %shard_map.116 = (f32[64,64,128]{2,1,0:T(8,128)}, f32[64,64,128]{2,1,0:T(8,128)}) custom-call(f32[64,64,128]{2,1,0:T(8,128)} %get-tuple-element.12.feat_a, f32[64,64,128]{2,1,0:T(8,128)} %get-tuple-element.13.feat_b, bf16[80,80,128]{2,1,0:T(8,128)(2,1)} %get-tuple-element.16.keys_a, bf16[80,80,128]{2,1,0:T(8,128)(2,1)} %get-tuple-element.17.keys_b, ...), custom_call_target="tpu_custom_call" | custom-call | tf_op jit(solution)/shard_map/pallas_call | solution.py:272

commit v2 on v1

--- a/solution.py
+++ b/solution.py
@@ -25,7 +25,7 @@
     rows, cols, channels = half_a.shape
     me = [lax.axis_index(axis) for axis in axes]
     counts = [lax.axis_size(axis) for axis in axes]
-    ways = [(dy, dx) for dy in (-1, 0, 1) for dx in (-1, 0, 1) if (dy, dx) != (0, 0)]
+    ways = [(0, -1), (0, 1), (-1, -1), (-1, 1), (1, -1), (1, 1), (-1, 0), (1, 0)]
 
     def present(way):
         there = [m + d for m, d in zip(me, way)]
@@ -82,7 +82,21 @@
             ext[R + row, pl.ds(R, cols), :] = half[row]
         return carry
 
-    lax.fori_loop(0, rows, move, 0)
+    lax.fori_loop(0, rows, move, 0, unroll=8)
+
+    for way in ways:
+        source = (-way[0], -way[1])
+
+        @pl.when(jnp.logical_not(present(source)))
+        def _(way=way):
+            (y, height), (x, width) = landing(way[0], rows), landing(way[1], cols)
+
+            def fill(row, carry):
+                for ext in (ext_a, ext_b):
+                    ext[row, pl.ds(x, width), :] = jnp.full((width, channels), EMPTY, ext.dtype)
+                return carry
+
+            lax.fori_loop(y, y + height, fill, 0)
 
     for i, way in enumerate(ways):
         source = (-way[0], -way[1])
@@ -96,17 +110,6 @@
         def _(i=i, way=way):
             copy(i, way, 0).wait_recv()
             copy(i, way, 1).wait_recv()
-
-        @pl.when(jnp.logical_not(present(source)))
-        def _(way=way):
-            (y, height), (x, width) = landing(way[0], rows), landing(way[1], cols)
-
-            def fill(row, carry):
-                for ext in (ext_a, ext_b):
-                    ext[row, pl.ds(x, width), :] = jnp.full((width, channels), EMPTY, ext.dtype)
-                return carry
-
-            lax.fori_loop(y, y + height, fill, 0)
 
 
 def halo(half_a, half_b, index):
@@ -183,7 +186,7 @@
                 lane_ref[row] = base + jnp.where(key[row] >= EMPTY, empty, zero)
             return carry
 
-        lax.fori_loop(0, keys_a.shape[0], fill, 0)
+        lax.fori_loop(0, keys_a.shape[0], fill, 0, unroll=8)
 
     def place(tile):
         tile = jnp.clip(tile, 0, count - 1)
@@ -258,7 +261,7 @@
 
 def one_pass(feats, keys, weights, halves):
     rows, cols, channels = feats[0].shape
-    height = 2 * band if rows % (2 * band) == 0 else band
+    height = next(k * band for k in (4, 2, 1) if rows % (k * band) == 0)
     strip = pl.BlockSpec((height, cols, channels), lambda i: (i, 0, 0))
     cells = band * tile_width
 

time: 110 us -> 107 us (0.973)
  Pallas kernels: 102 us -> 99.6 us
    pallas_call x2, Pallas kernels: 71.8 us -> 68.9 us  [one_pass(): pl.pallas_call(functools.partial(pass_kernel, halves=halves), grid=(rows...]
where the time goes in v2:
time: 107 us
  Pallas kernels  99.6 us (93%)
  other arithmetic  6.27 us (6%)
    pallas_call x2, Pallas kernels, one_pass(): pl.pallas_call(functools.partial(pass_kernel, halves=halves), grid=(rows...  68.9 us
    pallas_call x2, Pallas kernels, halo(): pl.pallas_call(functools.partial(halo_kernel, axes=('gy', 'gx')), out_sha...  30.7 us
    convert_element_type x1, other arithmetic, keyed(): return jnp.where(occ[..., None] > 0, feat, EMPTY).astype(jnp.bfloat16)  4.74 us

profile of v2, /device:TPU:3, one launch (start us, length us, event | category | flops | bytes accessed | tf_op | source)
XLA Modules:
  0.0 106.5 jit_solution(15756423987104982493)
XLA Ops:
  0.6 0.8 broadcast_compare_fusion.1
  1.4 0.8 broadcast_compare_fusion
  2.2 4.7 %select_convert_fusion = (bf16[64,64,128]{2,1,0:T(8,128)(2,1)}, bf16[64,64,128]{2,1,0:T(8,128)(2,1)}) fusion(f32[64,64,128]{2,1,0:T(8,128)} %feat_b.1, pred[64,64]{1,0:T(8,128)(4,1)S(1)} %broadcast_compare_fusion, f32[64,64,128]{2,1,0:T(8,128)} %feat_a.1, pred[64,64]{1,0:T(8,128)(4,1)S(1)} %broadcast_compare_fusion.1), kind=kLoop, calls=%fused_computation | loop fusion | flops 1048576 | bytes 6299648 | tf_op jit(solution)/shard_map/convert_element_type | solution.py:290
  6.9 15.7 %shard_map.113 = (bf16[80,80,128]{2,1,0:T(8,128)(2,1)}, bf16[80,80,128]{2,1,0:T(8,128)(2,1)}) custom-call(bf16[64,64,128]{2,1,0:T(8,128)(2,1)} %get-tuple-element.19.half_a, bf16[64,64,128]{2,1,0:T(8,128)(2,1)} %get-tuple-element.18.half_b), custom_call_target="tpu_custom_call" | custom-call | tf_op jit(solution)/shard_map/pallas_call | solution.py:118
  22.7 34.6 %shard_map.114 = (f32[64,64,128]{2,1,0:T(8,128)}, f32[64,64,128]{2,1,0:T(8,128)}, bf16[64,64,128]{2,1,0:T(8,128)(2,1)}, bf16[64,64,128]{2,1,0:T(8,128)(2,1)}) custom-call(f32[64,64,128]{2,1,0:T(8,128)} %feat_a.1, f32[64,64,128]{2,1,0:T(8,128)} %feat_b.1, bf16[80,80,128]{2,1,0:T(8,128)(2,1)} %get-tuple-element.10.keys_a, ...), custom_call_target="tpu_custom_call" | custom-call | tf_op jit(solution)/shard_map/pallas_call | solution.py:275
  57.3 15.0 %shard_map.115 = (bf16[80,80,128]{2,1,0:T(8,128)(2,1)}, bf16[80,80,128]{2,1,0:T(8,128)(2,1)}) custom-call(bf16[64,64,128]{2,1,0:T(8,128)(2,1)} %get-tuple-element.14.half_a, bf16[64,64,128]{2,1,0:T(8,128)(2,1)} %get-tuple-element.15.half_b), custom_call_target="tpu_custom_call" | custom-call | tf_op jit(solution)/shard_map/pallas_call | solution.py:118
  72.3 34.3 %shard_map.116 = (f32[64,64,128]{2,1,0:T(8,128)}, f32[64,64,128]{2,1,0:T(8,128)}) custom-call(f32[64,64,128]{2,1,0:T(8,128)} %get-tuple-element.12.feat_a, f32[64,64,128]{2,1,0:T(8,128)} %get-tuple-element.13.feat_b, bf16[80,80,128]{2,1,0:T(8,128)(2,1)} %get-tuple-element.16.keys_a, bf16[80,80,128]{2,1,0:T(8,128)(2,1)} %get-tuple-element.17.keys_b, ...), custom_call_target="tpu_custom_call" | custom-call | tf_op jit(solution)/shard_map/pallas_call | solution.py:275
